TPU v7x, 128 devices: a whole 4x4x4 slice. The times are simulated.
128 devices in a mesh: grp: 4 (over y), own: 32 (over x, z, core).
Axes of the slice: x: 4, y: 4, z: 4, core: 2. Of those that a mesh axis runs over, the one named last changes fastest.
Arguments:
- embeddings: float32 [98304, 768], P(('grp', 'own')), may hold values from -64 to 64
- cluster_ids: int32 [98304], P(('grp', 'own')), may hold values from 0 to 511, as said below
- owner_map: int32 [512], replicated, may hold values from 0 to 31, as said below
- source_order: int32 [98304], P(('grp', 'own')), may hold values from 0 to 767, as said below
Outputs:
- dup_score: float32 [98304], P(('grp', 'own'))
- centroids: float32 [512, 768], P('own')
Inputs may be any that keep to these rules, and one draw needn't show every extreme that they name: `owner_map`: every owner index is given to exactly 16 clusters. `cluster_ids`: within the 768 rows of one device, at most 48 rows have clusters of one owner index; in every draw some owner index receives exactly 48 rows from every device, and every device sends exactly 48 rows to some owner index. Cluster sizes are uneven and some clusters may be empty. `source_order`: each aligned block of 768 entries is a permutation of 0 to 767.
All inputs are finite; a program needn't handle non-finite values.
Results may differ from a plain program's by a relative error of at most 0.0003.
Values sent between devices are 32-bit elements; how exact they have to be, the bound alone decides.
A program may use at most 128 MiB of HBM per device.

v0:
```python
import jax
import jax.numpy as jnp
from jax import lax
from jax.sharding import PartitionSpec as P

CL_OWN = 16
sharpness = 6.0


def unit_rows(embeddings):
    squares = jnp.sum(embeddings * embeddings, axis=1, keepdims=True)
    return embeddings * lax.rsqrt(squares + 1e-06)


def owner_positions(owner_map):
    cluster_index = jnp.arange(owner_map.shape[0], dtype=jnp.int32)
    same_owner = owner_map[:, None] == owner_map[None, :]
    earlier = cluster_index[None, :] < cluster_index[:, None]
    before = jnp.sum((same_owner & earlier).astype(jnp.int32), axis=1)
    return owner_map * CL_OWN + before


def masked_weights(left_rows, left_ids, right_rows, right_ids):
    scores = jnp.einsum(
        "id,jd->ij",
        left_rows,
        right_rows,
        preferred_element_type=jnp.float32,
        precision=lax.Precision.HIGHEST,
    )
    linked = (left_ids[:, None] == right_ids[None, :]) & (left_ids[:, None] >= 0)
    return jnp.where(linked, jnp.exp(sharpness * (scores - 1.0)), 0.0)


def tile_sums(left_rows, left_ids, right_rows, right_ids):
    right_count = right_rows.shape[0]
    block_rows = 512
    block_count = right_count // block_rows
    right_blocks = right_rows.reshape(block_count, block_rows, right_rows.shape[1])
    id_blocks = right_ids.reshape(block_count, block_rows)

    def one_block(row_total, block_pair):
        weights = masked_weights(left_rows, left_ids, block_pair[0], block_pair[1])
        column_part = None
        return (row_total + jnp.sum(weights, axis=1), column_part)

    row_sums, column_sums = lax.scan(
        one_block, jnp.zeros((left_rows.shape[0],), jnp.float32), (right_blocks, id_blocks)
    )
    return (row_sums, column_sums)


def local(embeddings, cluster_ids, owner_map, source_order):
    row_count, feature_width = embeddings.shape
    owner_count = lax.axis_size("own")
    capacity = 2 * row_count // owner_count
    slot_count = owner_count * capacity
    cluster_count = owner_map.shape[0]
    unit_embed = unit_rows(embeddings)
    cluster_index = jnp.arange(cluster_count, dtype=jnp.int32)
    cluster_match = cluster_ids[:, None] == cluster_index[None, :]
    row_owner = jnp.sum(jnp.where(cluster_match, owner_map[None, :], 0), axis=1)
    owner_hot = (row_owner[:, None] == jnp.arange(owner_count, dtype=jnp.int32)[None, :]).astype(
        jnp.int32
    )
    rank_index = jnp.sum(jnp.cumsum(owner_hot, axis=0) * owner_hot, axis=1) - 1
    slot_index = row_owner * capacity + rank_index
    send_rows = jnp.zeros((slot_count, feature_width), jnp.float32).at[slot_index].set(unit_embed)
    send_ids = jnp.full((slot_count,), -1, jnp.int32).at[slot_index].set(cluster_ids)
    held_rows, held_ids = (
        lax.all_to_all(
            send_rows.reshape(owner_count, capacity, feature_width),
            "own",
            split_axis=0,
            concat_axis=0,
            tiled=True,
        ),
        lax.all_to_all(
            send_ids.reshape(owner_count, capacity), "own", split_axis=0, concat_axis=0, tiled=True
        ),
    )
    held_rows = held_rows.reshape(slot_count, feature_width)
    held_ids = held_ids.reshape(slot_count)
    row_sums, column_sums = tile_sums(
        held_rows,
        held_ids,
        lax.all_gather(held_rows, "grp", axis=0, tiled=True),
        lax.all_gather(held_ids, "grp", axis=0, tiled=True),
    )
    returned = lax.all_to_all(
        row_sums.reshape(owner_count, capacity), "own", split_axis=0, concat_axis=0, tiled=True
    )
    row_score = jnp.log(returned.reshape(slot_count)[slot_index])
    dup_score = jnp.zeros((row_count,), jnp.float32).at[source_order].set(row_score)
    position = owner_positions(owner_map)
    position_index = jnp.arange(cluster_count, dtype=jnp.int32)
    ordered = jnp.sum(
        jnp.where(position[None, :] == position_index[:, None], cluster_index[None, :], 0), axis=1
    )
    cluster_hot = (cluster_ids[:, None] == ordered[None, :]).astype(jnp.float32)
    cluster_terms = lax.dot_general(
        cluster_hot,
        unit_embed,
        (((0,), (0,)), ((), ())),
        preferred_element_type=jnp.float32,
        precision=lax.Precision.HIGHEST,
    )
    partial_value = lax.psum_scatter(cluster_terms, "own", scatter_dimension=0, tiled=True)
    cluster_sums = lax.psum(partial_value, "grp")
    centroids = cluster_sums * lax.rsqrt(
        jnp.mean(cluster_sums * cluster_sums, axis=1, keepdims=True) + 1e-06
    )
    return (dup_score, centroids)


def solution(mesh):
    placed = (P(("grp", "own"), None), P(("grp", "own")), P(), P(("grp", "own")))
    return jax.shard_map(
        local,
        mesh=mesh,
        in_specs=placed,
        out_specs=(P(("grp", "own")), P("own", None)),
        check_vma=False,
    )
```

profile of v0, /device:TPU:1, one launch (start us, length us, event | category | flops | bytes accessed | tf_op | source)
XLA Modules:
  0.0 433.6 jit_solution(5770465693371880921)
XLA Ops:
  8.0 1.2 select_reduce_fusion
  9.2 1.7 reduce-window.6
  11.4 1.9 multiply_reduce_fusion
  13.3 9.7 %scatter_custom_fusion.1 = f32[1536,768]{1,0:T(8,128)} fusion(s32[768]{0:T(1024)S(1)} %fusion.26, f32[]{:T(128)} %constant.55.clone.1, f32[768,768]{1,0:T(8,128)S(1)} %copy-done, f32[768]{0:T(1024)S(1)} %add_rsqrt_fusion), kind=kCustom, calls=%fused_computation.17 | custom fusion | flops 589824 | bytes 7081988 | tf_op jit(solution)/shard_map/scatter | solution.py:68
  23.1 9.6 %all-to-all-start.1 = ((f32[32,48,768]{2,1,0:T(8,128)}), f32[32,48,768]{2,1,0:T(8,128)}, u32[]{:S(2)}, u32[]{:S(2)}) async-start(f32[32,48,768]{2,1,0:T(8,128)} %bitcast.46), calls=%async_computation.1 | async-start | bytes 9437184 | tf_op jit(solution)/shard_map/all_to_all | solution.py:71
  33.2 3.8 fusion.12
  37.1 55.2 %all-to-all-done.1 = f32[32,48,768]{2,1,0:T(8,128)} async-done(((f32[32,48,768]{2,1,0:T(8,128)}), f32[32,48,768]{2,1,0:T(8,128)}, u32[]{:S(2)}, u32[]{:S(2)}) %all-to-all-start.1) | async-done | bytes 4718624 | tf_op jit(solution)/shard_map/all_to_all | solution.py:71
  92.3 3.4 scatter_custom_fusion
  95.7 0.7 all_to_all.17
  96.4 9.8 %all-to-all-start = ((s32[32,1,48]{2,1,0:T(1,128)}), s32[32,1,48]{2,1,0:T(1,128)S(1)}, u32[]{:S(2)}, u32[]{:S(2)}) async-start(s32[32,1,48]{2,1,0:T(1,128)} %all_to_all.17), calls=%async_computation | async-start | bytes 32768 | tf_op jit(solution)/shard_map/all_to_all | solution.py:78
  106.2 6.8 %all-to-all-done = s32[32,1,48]{2,1,0:T(1,128)S(1)} async-done(((s32[32,1,48]{2,1,0:T(1,128)}), s32[32,1,48]{2,1,0:T(1,128)S(1)}, u32[]{:S(2)}, u32[]{:S(2)}) %all-to-all-start) | async-done | bytes 6176 | tf_op jit(solution)/shard_map/all_to_all | solution.py:78
  114.4 10.7 %all-gather = s32[4,1,1536]{2,1,0:T(1,128)S(1)} all-gather(s32[1,1,1536]{2,1,0:T(1,128)S(1)} %reshape.149), channel_id=1, replica_groups=mesh['grp'=4,'own'=32] {'grp'}, dimensions={0}, use_global_device_ids=true | all-gather | bytes 30720 | tf_op jit(solution)/shard_map/all_gather | solution.py:88
  125.1 16.3 %psum.7 = f32[16,768]{1,0:T(8,128)S(1)} all-reduce(f32[16,768]{1,0:T(8,128)} %reduce-scatter.2.cloned.1.call-done), channel_id=1, replica_groups=mesh['grp'=4,'own'=32] {'grp'}, use_global_device_ids=true, to_apply=%region_14.15 | all-reduce | flops 12288 | bytes 98304 | tf_op jit(solution)/shard_map/psum | solution.py:109
  141.6 127.8 %all-gather.3.cloned.1.call-done = f32[6144,768]{1,0:T(8,128)} async-done(((f32[1536,768]{1,0:T(8,128)}), f32[6144,768]{1,0:T(8,128)}) %all-gather.3.cloned.1.call-update) | async-done | bytes 18874384 | tf_op jit(solution)/shard_map/all_gather | solution.py:87
  269.4 131.6 %while.14 = (s32[]{:T(128)}, f32[1536]{0:T(1024)S(1)}, s32[32,48]{1,0:T(8,128)}, s32[12,512]{1,0:T(8,128)S(1)}, f32[12,512,768]{2,1,0:T(8,128)}, /*index=5*/f32[...) while((s32[]{:T(128)}, f32[1536]{0:T(1024)S(1)}, s32[32,48]{1,0:T(8,128)}, ...), condition=%wide.wide.region_9.10_spmd.clone, body=%wide.wide.region_7.9_spmd.clone.sunk | while | flops 7252478976 | bytes 6338155 | solution.py:47
  269.4 10.9 %fusion.38 = f32[1536]{0:T(1024)S(1)} fusion(f32[1536,768]{1,0:T(8,128)} %get-tuple-element.203, f32[12,512,768]{2,1,0:T(8,128)} %get-tuple-element.202, s32[]{:T(128)} %get-tuple-element.189, pred[1536]{0:T(1024)(128)(4,1)S(1)} %broadcast_compare_fusion.3, s32[512]{0:T(512)S(1)} %bitcast.50, s32[1536]{0:T(1024)S(1)} %get-tuple-element.204), kind=kOutput, calls=%fused_computation.11.clone.clone.1 | convolution fusion | flops 7252474368 | bytes 6307840 | tf_op jit(solution)/shard_map/while/body/eval_jaxpr/id,jd->ij/dot_general | solution.py:24
  280.4 10.9 %fusion.38 = f32[1536]{0:T(1024)S(1)} fusion(f32[1536,768]{1,0:T(8,128)} %get-tuple-element.203, f32[12,512,768]{2,1,0:T(8,128)} %get-tuple-element.202, s32[]{:T(128)} %get-tuple-element.189, pred[1536]{0:T(1024)(128)(4,1)S(1)} %broadcast_compare_fusion.3, s32[512]{0:T(512)S(1)} %bitcast.50, s32[1536]{0:T(1024)S(1)} %get-tuple-element.204), kind=kOutput, calls=%fused_computation.11.clone.clone.1 | convolution fusion | flops 7252474368 | bytes 6307840 | tf_op jit(solution)/shard_map/while/body/eval_jaxpr/id,jd->ij/dot_general | solution.py:24
  291.4 10.9 %fusion.38 = f32[1536]{0:T(1024)S(1)} fusion(f32[1536,768]{1,0:T(8,128)} %get-tuple-element.203, f32[12,512,768]{2,1,0:T(8,128)} %get-tuple-element.202, s32[]{:T(128)} %get-tuple-element.189, pred[1536]{0:T(1024)(128)(4,1)S(1)} %broadcast_compare_fusion.3, s32[512]{0:T(512)S(1)} %bitcast.50, s32[1536]{0:T(1024)S(1)} %get-tuple-element.204), kind=kOutput, calls=%fused_computation.11.clone.clone.1 | convolution fusion | flops 7252474368 | bytes 6307840 | tf_op jit(solution)/shard_map/while/body/eval_jaxpr/id,jd->ij/dot_general | solution.py:24
  302.3 10.9 %fusion.38 = f32[1536]{0:T(1024)S(1)} fusion(f32[1536,768]{1,0:T(8,128)} %get-tuple-element.203, f32[12,512,768]{2,1,0:T(8,128)} %get-tuple-element.202, s32[]{:T(128)} %get-tuple-element.189, pred[1536]{0:T(1024)(128)(4,1)S(1)} %broadcast_compare_fusion.3, s32[512]{0:T(512)S(1)} %bitcast.50, s32[1536]{0:T(1024)S(1)} %get-tuple-element.204), kind=kOutput, calls=%fused_computation.11.clone.clone.1 | convolution fusion | flops 7252474368 | bytes 6307840 | tf_op jit(solution)/shard_map/while/body/eval_jaxpr/id,jd->ij/dot_general | solution.py:24
  313.3 10.9 %fusion.38 = f32[1536]{0:T(1024)S(1)} fusion(f32[1536,768]{1,0:T(8,128)} %get-tuple-element.203, f32[12,512,768]{2,1,0:T(8,128)} %get-tuple-element.202, s32[]{:T(128)} %get-tuple-element.189, pred[1536]{0:T(1024)(128)(4,1)S(1)} %broadcast_compare_fusion.3, s32[512]{0:T(512)S(1)} %bitcast.50, s32[1536]{0:T(1024)S(1)} %get-tuple-element.204), kind=kOutput, calls=%fused_computation.11.clone.clone.1 | convolution fusion | flops 7252474368 | bytes 6307840 | tf_op jit(solution)/shard_map/while/body/eval_jaxpr/id,jd->ij/dot_general | solution.py:24
  324.3 10.9 %fusion.38 = f32[1536]{0:T(1024)S(1)} fusion(f32[1536,768]{1,0:T(8,128)} %get-tuple-element.203, f32[12,512,768]{2,1,0:T(8,128)} %get-tuple-element.202, s32[]{:T(128)} %get-tuple-element.189, pred[1536]{0:T(1024)(128)(4,1)S(1)} %broadcast_compare_fusion.3, s32[512]{0:T(512)S(1)} %bitcast.50, s32[1536]{0:T(1024)S(1)} %get-tuple-element.204), kind=kOutput, calls=%fused_computation.11.clone.clone.1 | convolution fusion | flops 7252474368 | bytes 6307840 | tf_op jit(solution)/shard_map/while/body/eval_jaxpr/id,jd->ij/dot_general | solution.py:24
  335.3 10.9 %fusion.38 = f32[1536]{0:T(1024)S(1)} fusion(f32[1536,768]{1,0:T(8,128)} %get-tuple-element.203, f32[12,512,768]{2,1,0:T(8,128)} %get-tuple-element.202, s32[]{:T(128)} %get-tuple-element.189, pred[1536]{0:T(1024)(128)(4,1)S(1)} %broadcast_compare_fusion.3, s32[512]{0:T(512)S(1)} %bitcast.50, s32[1536]{0:T(1024)S(1)} %get-tuple-element.204), kind=kOutput, calls=%fused_computation.11.clone.clone.1 | convolution fusion | flops 7252474368 | bytes 6307840 | tf_op jit(solution)/shard_map/while/body/eval_jaxpr/id,jd->ij/dot_general | solution.py:24
  346.2 10.9 %fusion.38 = f32[1536]{0:T(1024)S(1)} fusion(f32[1536,768]{1,0:T(8,128)} %get-tuple-element.203, f32[12,512,768]{2,1,0:T(8,128)} %get-tuple-element.202, s32[]{:T(128)} %get-tuple-element.189, pred[1536]{0:T(1024)(128)(4,1)S(1)} %broadcast_compare_fusion.3, s32[512]{0:T(512)S(1)} %bitcast.50, s32[1536]{0:T(1024)S(1)} %get-tuple-element.204), kind=kOutput, calls=%fused_computation.11.clone.clone.1 | convolution fusion | flops 7252474368 | bytes 6307840 | tf_op jit(solution)/shard_map/while/body/eval_jaxpr/id,jd->ij/dot_general | solution.py:24
  357.2 10.9 %fusion.38 = f32[1536]{0:T(1024)S(1)} fusion(f32[1536,768]{1,0:T(8,128)} %get-tuple-element.203, f32[12,512,768]{2,1,0:T(8,128)} %get-tuple-element.202, s32[]{:T(128)} %get-tuple-element.189, pred[1536]{0:T(1024)(128)(4,1)S(1)} %broadcast_compare_fusion.3, s32[512]{0:T(512)S(1)} %bitcast.50, s32[1536]{0:T(1024)S(1)} %get-tuple-element.204), kind=kOutput, calls=%fused_computation.11.clone.clone.1 | convolution fusion | flops 7252474368 | bytes 6307840 | tf_op jit(solution)/shard_map/while/body/eval_jaxpr/id,jd->ij/dot_general | solution.py:24
  368.2 10.9 %fusion.38 = f32[1536]{0:T(1024)S(1)} fusion(f32[1536,768]{1,0:T(8,128)} %get-tuple-element.203, f32[12,512,768]{2,1,0:T(8,128)} %get-tuple-element.202, s32[]{:T(128)} %get-tuple-element.189, pred[1536]{0:T(1024)(128)(4,1)S(1)} %broadcast_compare_fusion.3, s32[512]{0:T(512)S(1)} %bitcast.50, s32[1536]{0:T(1024)S(1)} %get-tuple-element.204), kind=kOutput, calls=%fused_computation.11.clone.clone.1 | convolution fusion | flops 7252474368 | bytes 6307840 | tf_op jit(solution)/shard_map/while/body/eval_jaxpr/id,jd->ij/dot_general | solution.py:24
  379.1 10.9 %fusion.38 = f32[1536]{0:T(1024)S(1)} fusion(f32[1536,768]{1,0:T(8,128)} %get-tuple-element.203, f32[12,512,768]{2,1,0:T(8,128)} %get-tuple-element.202, s32[]{:T(128)} %get-tuple-element.189, pred[1536]{0:T(1024)(128)(4,1)S(1)} %broadcast_compare_fusion.3, s32[512]{0:T(512)S(1)} %bitcast.50, s32[1536]{0:T(1024)S(1)} %get-tuple-element.204), kind=kOutput, calls=%fused_computation.11.clone.clone.1 | convolution fusion | flops 7252474368 | bytes 6307840 | tf_op jit(solution)/shard_map/while/body/eval_jaxpr/id,jd->ij/dot_general | solution.py:24
  390.1 10.9 %fusion.38 = f32[1536]{0:T(1024)S(1)} fusion(f32[1536,768]{1,0:T(8,128)} %get-tuple-element.203, f32[12,512,768]{2,1,0:T(8,128)} %get-tuple-element.202, s32[]{:T(128)} %get-tuple-element.189, pred[1536]{0:T(1024)(128)(4,1)S(1)} %broadcast_compare_fusion.3, s32[512]{0:T(512)S(1)} %bitcast.50, s32[1536]{0:T(1024)S(1)} %get-tuple-element.204), kind=kOutput, calls=%fused_computation.11.clone.clone.1 | convolution fusion | flops 7252474368 | bytes 6307840 | tf_op jit(solution)/shard_map/while/body/eval_jaxpr/id,jd->ij/dot_general | solution.py:24
  401.7 7.7 %all-to-all-start.2 = ((f32[32,1,48]{2,1,0:T(1,128)}), f32[32,1,48]{2,1,0:T(1,128)S(1)}, u32[]{:S(2)}, u32[]{:S(2)}) async-start(f32[32,1,48]{2,1,0:T(1,128)} %all_to_all.21), calls=%async_computation.2 | async-start | bytes 32768 | tf_op jit(solution)/shard_map/all_to_all | solution.py:90
  409.5 0.7 broadcast_multiply_fusion
  410.2 6.2 %all-to-all-done.2 = f32[32,1,48]{2,1,0:T(1,128)S(1)} async-done(((f32[32,1,48]{2,1,0:T(1,128)}), f32[32,1,48]{2,1,0:T(1,128)S(1)}, u32[]{:S(2)}, u32[]{:S(2)}) %all-to-all-start.2) | async-done | bytes 6176 | tf_op jit(solution)/shard_map/all_to_all | solution.py:90
  417.7 4.5 %gather_fusion = f32[768]{0:T(1024)S(1)} fusion(f32[1536]{0:T(1024)S(1)} %reshape.115, s32[1024]{0:T(1024)S(1)} %pad_clamp_fusion), kind=kCustom, calls=%fused_computation | custom fusion | bytes 9216 | tf_op jit(solution)/shard_map/gather | solution.py:93
  422.2 3.9 scatter_custom_fusion.2
  (77 shorter events, 4.8 us)
Async XLA Ops:
  8.0 5.3 %copy-start = (f32[768,768]{1,0:T(8,128)S(1)}, f32[768,768]{1,0:T(8,128)}, u32[]{:S(2)}) copy-start(f32[768,768]{1,0:T(8,128)} %param.6) | copy-start | bytes 7077892
  23.1 9.7 %copy-start.2 = (s32[512]{0:T(512)S(1)}, s32[512]{0:T(512)}, u32[]{:S(2)}) copy-start(s32[512]{0:T(512)} %param.8) | copy-start | bytes 6148
  23.1 10.1 %copy-start.3 = (s32[768]{0:T(1024)S(1)}, s32[768]{0:T(1024)}, u32[]{:S(2)}) copy-start(s32[768]{0:T(1024)} %param.7) | copy-start | bytes 9220
  23.1 69.2 %all-to-all-start.1 = ((f32[32,48,768]{2,1,0:T(8,128)}), f32[32,48,768]{2,1,0:T(8,128)}, u32[]{:S(2)}, u32[]{:S(2)}) async-start(f32[32,48,768]{2,1,0:T(8,128)} %bitcast.46), calls=%async_computation.1 | async-start | bytes 9437184 | tf_op jit(solution)/shard_map/all_to_all | solution.py:71
  32.7 92.4 %reduce-scatter.2.cloned.1.call-start = ((), (), s32[]{:S(2)}) async-start(), calls=%async_computation.5 | async-start | bytes 1622016 | tf_op jit(solution)/shard_map/reduce_scatter | solution.py:108
  37.0 232.4 %all-gather.3.cloned.1.call-start = ((), (), s32[]{:S(2)}) async-start(), calls=%async_computation.4 | async-start | bytes 23592960 | tf_op jit(solution)/shard_map/all_gather | solution.py:87
  92.3 13.9 %copy-start.4 = (s32[768]{0:T(1024)S(1)}, s32[768]{0:T(1024)}, u32[]{:S(2)}) copy-start(s32[768]{0:T(1024)} %param.9) | copy-start | bytes 9220
  96.4 16.6 %all-to-all-start = ((s32[32,1,48]{2,1,0:T(1,128)}), s32[32,1,48]{2,1,0:T(1,128)S(1)}, u32[]{:S(2)}, u32[]{:S(2)}) async-start(s32[32,1,48]{2,1,0:T(1,128)} %all_to_all.17), calls=%async_computation | async-start | bytes 32768 | tf_op jit(solution)/shard_map/all_to_all | solution.py:78
  113.1 156.3 %copy-start.1 = (s32[32,1,48]{2,1,0:T(1,128)}, s32[32,1,48]{2,1,0:T(1,128)S(1)}, u32[]{:S(2)}) copy-start(s32[32,1,48]{2,1,0:T(1,128)S(1)} %all-to-all-done) | copy-start | bytes 18436
  401.7 14.7 %all-to-all-start.2 = ((f32[32,1,48]{2,1,0:T(1,128)}), f32[32,1,48]{2,1,0:T(1,128)S(1)}, u32[]{:S(2)}, u32[]{:S(2)}) async-start(f32[32,1,48]{2,1,0:T(1,128)} %all_to_all.21), calls=%async_computation.2 | async-start | bytes 32768 | tf_op jit(solution)/shard_map/all_to_all | solution.py:90
Sparse Core Ops, SparseCore 0:
  37.1 80.2 reduce-scatter.1
Sparse Core Ops, SparseCore 1:
  92.4 176.9 all-gather.2
where the time goes:
time: 434 us
  waiting for transfers between devices  196 us (45%)
  matrix products  135 us (31%)
  starting transfers between devices  27.2 us (6%)
  blocking collectives  27 us (6%)
  other arithmetic  17.5 us (4%)
  between operations  15.7 us (4%)
  local copies, waits for them, and re-layouts  14.8 us (3%)
    dot_general x12, matrix products, masked_weights(): jnp.einsum('id,jd->ij', left_rows, right_rows, preferred_element_type=jnp...  131 us
    all_gather x1, waiting for transfers between devices, local(): lax.all_gather(held_rows, 'grp', axis=0, tiled=True)  128 us
    all_to_all x1, waiting for transfers between devices, local(): lax.all_to_all(send_rows.reshape(owner_count, capacity, feature_width), '...  55.2 us
    psum x1, blocking collectives, local(): cluster_sums = lax.psum(partial_value, 'grp')  16.3 us
    all_gather x1, blocking collectives, local(): lax.all_gather(held_ids, 'grp', axis=0, tiled=True)  10.7 us
    all_to_all x1, starting transfers between devices, local(): lax.all_to_all(send_ids.reshape(owner_count, capacity), 'own', split_axis...  9.77 us
    scatter x1, other arithmetic, local(): jnp.zeros((slot_count, feature_width), jnp.float32).at[slot_index]  9.72 us
    all_to_all x1, starting transfers between devices, local(): lax.all_to_all(send_rows.reshape(owner_count, capacity, feature_width), '...  9.61 us
  transfers between devices with their start and end apart: 5, of which 4 were waited for; matrix products, arithmetic and copies ran while one was open for 2% of the time, Pallas kernels for 0%

commit v1 on v0

--- a/solution.py
+++ b/solution.py
@@ -106,7 +106,11 @@
         precision=lax.Precision.HIGHEST,
     )
     partial_value = lax.psum_scatter(cluster_terms, "own", scatter_dimension=0, tiled=True)
-    cluster_sums = lax.psum(partial_value, "grp")
+    cluster_sums = partial_value
+    for hop in (1, 2):
+        cluster_sums = cluster_sums + lax.ppermute(
+            cluster_sums, "grp", [(dev, dev ^ hop) for dev in range(4)]
+        )
     centroids = cluster_sums * lax.rsqrt(
         jnp.mean(cluster_sums * cluster_sums, axis=1, keepdims=True) + 1e-06
     )

time: 434 us -> 434 us (level)
  blocking collectives: 27 us -> 10.4 us
  waiting for transfers between devices: 196 us -> 208 us
    psum x1 -> x0, blocking collectives: 16.3 us -> none  [local(): cluster_sums = lax.psum(partial_value, 'grp')]
    reduce_scatter x1, waiting for transfers between devices: 0.02 us -> 11.3 us  [local(): lax.psum_scatter(cluster_terms, 'own', scatter_dimension=0, tiled=True)]
    all_to_all x1, waiting for transfers between devices: 6.82 us -> 0.01 us  [local(): lax.all_to_all(send_ids.reshape(owner_count, capacity), 'own', split_axis...]
  transfers between devices with their start and end apart: 5 -> 7, of which waited for: 4 -> 5; matrix products, arithmetic and copies ran while one was open for 2% -> 2% of each run, Pallas kernels for 0% -> 0%
where the time goes in v1:
time: 434 us
  waiting for transfers between devices  208 us (48%)
  matrix products  135 us (31%)
  starting transfers between devices  31.2 us (7%)
  other arithmetic  18.3 us (4%)
  between operations  15.7 us (4%)
  local copies, waits for them, and re-layouts  14.9 us (3%)
  blocking collectives  10.4 us (2%)
    all_gather x1, waiting for transfers between devices, local(): lax.all_gather(held_rows, 'grp', axis=0, tiled=True)  132 us
    dot_general x12, matrix products, masked_weights(): jnp.einsum('id,jd->ij', left_rows, right_rows, preferred_element_type=jnp...  131 us
    all_to_all x1, waiting for transfers between devices, local(): lax.all_to_all(send_rows.reshape(owner_count, capacity, feature_width), '...  55.2 us
    reduce_scatter x1, waiting for transfers between devices, local(): lax.psum_scatter(cluster_terms, 'own', scatter_dimension=0, tiled=True)  11.3 us
    all_gather x1, blocking collectives, local(): lax.all_gather(held_ids, 'grp', axis=0, tiled=True)  10.4 us
    all_to_all x1, starting transfers between devices, local(): lax.all_to_all(send_ids.reshape(owner_count, capacity), 'own', split_axis...  9.77 us
    scatter x1, other arithmetic, local(): jnp.zeros((slot_count, feature_width), jnp.float32).at[slot_index]  9.72 us
    all_to_all x1, starting transfers between devices, local(): lax.all_to_all(send_rows.reshape(owner_count, capacity, feature_width), '...  9.61 us
  transfers between devices with their start and end apart: 7, of which 5 were waited for; matrix products, arithmetic and copies ran while one was open for 2% of the time, Pallas kernels for 0%

profile of v1, /device:TPU:1, one launch (start us, length us, event | category | flops | bytes accessed | tf_op | source)
XLA Modules:
  0.0 433.7 jit_solution(16509298002678625688)
XLA Ops:
  8.0 1.2 select_reduce_fusion
  9.2 1.7 reduce-window.6
  11.4 1.9 multiply_reduce_fusion
  13.3 9.7 %scatter_custom_fusion.1 = f32[1536,768]{1,0:T(8,128)} fusion(s32[768]{0:T(1024)S(1)} %fusion.26, f32[]{:T(128)} %constant.55.clone.1, f32[768,768]{1,0:T(8,128)S(1)} %copy-done, f32[768]{0:T(1024)S(1)} %add_rsqrt_fusion), kind=kCustom, calls=%fused_computation.17 | custom fusion | flops 589824 | bytes 7081988 | tf_op jit(solution)/shard_map/scatter | solution.py:68
  23.1 9.6 %all-to-all-start.1 = ((f32[32,48,768]{2,1,0:T(8,128)}), f32[32,48,768]{2,1,0:T(8,128)}, u32[]{:S(2)}, u32[]{:S(2)}) async-start(f32[32,48,768]{2,1,0:T(8,128)} %bitcast.46), calls=%async_computation.1 | async-start | bytes 9437184 | tf_op jit(solution)/shard_map/all_to_all | solution.py:71
  33.2 3.8 fusion.12
  37.1 55.2 %all-to-all-done.1 = f32[32,48,768]{2,1,0:T(8,128)} async-done(((f32[32,48,768]{2,1,0:T(8,128)}), f32[32,48,768]{2,1,0:T(8,128)}, u32[]{:S(2)}, u32[]{:S(2)}) %all-to-all-start.1) | async-done | bytes 4718624 | tf_op jit(solution)/shard_map/all_to_all | solution.py:71
  92.3 3.4 scatter_custom_fusion
  96.4 9.8 %all-to-all-start = ((s32[32,1,48]{2,1,0:T(1,128)}), s32[32,1,48]{2,1,0:T(1,128)S(1)}, u32[]{:S(2)}, u32[]{:S(2)}) async-start(s32[32,1,48]{2,1,0:T(1,128)} %all_to_all.17), calls=%async_computation | async-start | bytes 32768 | tf_op jit(solution)/shard_map/all_to_all | solution.py:78
  106.2 11.3 %reduce-scatter.2.cloned.1.call-done = f32[16,768]{1,0:T(8,128)} async-done(((f32[512,768]{1,0:T(8,128)}), f32[16,768]{1,0:T(8,128)}) %reduce-scatter.2.cloned.1.call-update) | async-done | bytes 49168 | tf_op jit(solution)/shard_map/reduce_scatter | solution.py:108
  117.5 1.2 collective-permute-start
  118.7 3.4 collective-permute-done
  122.8 2.7 collective-permute-start.1
  126.8 10.4 %all-gather = s32[4,1,1536]{2,1,0:T(1,128)S(1)} all-gather(s32[1,1,1536]{2,1,0:T(1,128)S(1)} %reshape.149), channel_id=1, replica_groups=mesh['grp'=4,'own'=32] {'grp'}, dimensions={0}, use_global_device_ids=true | all-gather | bytes 30720 | tf_op jit(solution)/shard_map/all_gather | solution.py:88
  137.4 132.1 %all-gather.3.cloned.1.call-done = f32[6144,768]{1,0:T(8,128)} async-done(((f32[1536,768]{1,0:T(8,128)}), f32[6144,768]{1,0:T(8,128)}) %all-gather.3.cloned.1.call-update) | async-done | bytes 18874384 | tf_op jit(solution)/shard_map/all_gather | solution.py:87
  269.5 131.6 %while.14 = (s32[]{:T(128)}, f32[1536]{0:T(1024)S(1)}, s32[32,48]{1,0:T(8,128)}, s32[12,512]{1,0:T(8,128)S(1)}, f32[12,512,768]{2,1,0:T(8,128)}, /*index=5*/f32[...) while((s32[]{:T(128)}, f32[1536]{0:T(1024)S(1)}, s32[32,48]{1,0:T(8,128)}, ...), condition=%wide.wide.region_9.10_spmd.clone, body=%wide.wide.region_7.9_spmd.clone.sunk | while | flops 7252478976 | bytes 6338155 | solution.py:47
  269.5 10.9 %fusion.38 = f32[1536]{0:T(1024)S(1)} fusion(f32[1536,768]{1,0:T(8,128)} %get-tuple-element.205, f32[12,512,768]{2,1,0:T(8,128)} %get-tuple-element.204, s32[]{:T(128)} %get-tuple-element.191, pred[1536]{0:T(1024)(128)(4,1)S(1)} %broadcast_compare_fusion.3, s32[512]{0:T(512)S(1)} %bitcast.50, s32[1536]{0:T(1024)S(1)} %get-tuple-element.206), kind=kOutput, calls=%fused_computation.11.clone.clone.1 | convolution fusion | flops 7252474368 | bytes 6307840 | tf_op jit(solution)/shard_map/while/body/eval_jaxpr/id,jd->ij/dot_general | solution.py:24
  280.5 10.9 %fusion.38 = f32[1536]{0:T(1024)S(1)} fusion(f32[1536,768]{1,0:T(8,128)} %get-tuple-element.205, f32[12,512,768]{2,1,0:T(8,128)} %get-tuple-element.204, s32[]{:T(128)} %get-tuple-element.191, pred[1536]{0:T(1024)(128)(4,1)S(1)} %broadcast_compare_fusion.3, s32[512]{0:T(512)S(1)} %bitcast.50, s32[1536]{0:T(1024)S(1)} %get-tuple-element.206), kind=kOutput, calls=%fused_computation.11.clone.clone.1 | convolution fusion | flops 7252474368 | bytes 6307840 | tf_op jit(solution)/shard_map/while/body/eval_jaxpr/id,jd->ij/dot_general | solution.py:24
  291.5 10.9 %fusion.38 = f32[1536]{0:T(1024)S(1)} fusion(f32[1536,768]{1,0:T(8,128)} %get-tuple-element.205, f32[12,512,768]{2,1,0:T(8,128)} %get-tuple-element.204, s32[]{:T(128)} %get-tuple-element.191, pred[1536]{0:T(1024)(128)(4,1)S(1)} %broadcast_compare_fusion.3, s32[512]{0:T(512)S(1)} %bitcast.50, s32[1536]{0:T(1024)S(1)} %get-tuple-element.206), kind=kOutput, calls=%fused_computation.11.clone.clone.1 | convolution fusion | flops 7252474368 | bytes 6307840 | tf_op jit(solution)/shard_map/while/body/eval_jaxpr/id,jd->ij/dot_general | solution.py:24
  302.4 10.9 %fusion.38 = f32[1536]{0:T(1024)S(1)} fusion(f32[1536,768]{1,0:T(8,128)} %get-tuple-element.205, f32[12,512,768]{2,1,0:T(8,128)} %get-tuple-element.204, s32[]{:T(128)} %get-tuple-element.191, pred[1536]{0:T(1024)(128)(4,1)S(1)} %broadcast_compare_fusion.3, s32[512]{0:T(512)S(1)} %bitcast.50, s32[1536]{0:T(1024)S(1)} %get-tuple-element.206), kind=kOutput, calls=%fused_computation.11.clone.clone.1 | convolution fusion | flops 7252474368 | bytes 6307840 | tf_op jit(solution)/shard_map/while/body/eval_jaxpr/id,jd->ij/dot_general | solution.py:24
  313.4 10.9 %fusion.38 = f32[1536]{0:T(1024)S(1)} fusion(f32[1536,768]{1,0:T(8,128)} %get-tuple-element.205, f32[12,512,768]{2,1,0:T(8,128)} %get-tuple-element.204, s32[]{:T(128)} %get-tuple-element.191, pred[1536]{0:T(1024)(128)(4,1)S(1)} %broadcast_compare_fusion.3, s32[512]{0:T(512)S(1)} %bitcast.50, s32[1536]{0:T(1024)S(1)} %get-tuple-element.206), kind=kOutput, calls=%fused_computation.11.clone.clone.1 | convolution fusion | flops 7252474368 | bytes 6307840 | tf_op jit(solution)/shard_map/while/body/eval_jaxpr/id,jd->ij/dot_general | solution.py:24
  324.4 10.9 %fusion.38 = f32[1536]{0:T(1024)S(1)} fusion(f32[1536,768]{1,0:T(8,128)} %get-tuple-element.205, f32[12,512,768]{2,1,0:T(8,128)} %get-tuple-element.204, s32[]{:T(128)} %get-tuple-element.191, pred[1536]{0:T(1024)(128)(4,1)S(1)} %broadcast_compare_fusion.3, s32[512]{0:T(512)S(1)} %bitcast.50, s32[1536]{0:T(1024)S(1)} %get-tuple-element.206), kind=kOutput, calls=%fused_computation.11.clone.clone.1 | convolution fusion | flops 7252474368 | bytes 6307840 | tf_op jit(solution)/shard_map/while/body/eval_jaxpr/id,jd->ij/dot_general | solution.py:24
  335.3 10.9 %fusion.38 = f32[1536]{0:T(1024)S(1)} fusion(f32[1536,768]{1,0:T(8,128)} %get-tuple-element.205, f32[12,512,768]{2,1,0:T(8,128)} %get-tuple-element.204, s32[]{:T(128)} %get-tuple-element.191, pred[1536]{0:T(1024)(128)(4,1)S(1)} %broadcast_compare_fusion.3, s32[512]{0:T(512)S(1)} %bitcast.50, s32[1536]{0:T(1024)S(1)} %get-tuple-element.206), kind=kOutput, calls=%fused_computation.11.clone.clone.1 | convolution fusion | flops 7252474368 | bytes 6307840 | tf_op jit(solution)/shard_map/while/body/eval_jaxpr/id,jd->ij/dot_general | solution.py:24
  346.3 10.9 %fusion.38 = f32[1536]{0:T(1024)S(1)} fusion(f32[1536,768]{1,0:T(8,128)} %get-tuple-element.205, f32[12,512,768]{2,1,0:T(8,128)} %get-tuple-element.204, s32[]{:T(128)} %get-tuple-element.191, pred[1536]{0:T(1024)(128)(4,1)S(1)} %broadcast_compare_fusion.3, s32[512]{0:T(512)S(1)} %bitcast.50, s32[1536]{0:T(1024)S(1)} %get-tuple-element.206), kind=kOutput, calls=%fused_computation.11.clone.clone.1 | convolution fusion | flops 7252474368 | bytes 6307840 | tf_op jit(solution)/shard_map/while/body/eval_jaxpr/id,jd->ij/dot_general | solution.py:24
  357.3 10.9 %fusion.38 = f32[1536]{0:T(1024)S(1)} fusion(f32[1536,768]{1,0:T(8,128)} %get-tuple-element.205, f32[12,512,768]{2,1,0:T(8,128)} %get-tuple-element.204, s32[]{:T(128)} %get-tuple-element.191, pred[1536]{0:T(1024)(128)(4,1)S(1)} %broadcast_compare_fusion.3, s32[512]{0:T(512)S(1)} %bitcast.50, s32[1536]{0:T(1024)S(1)} %get-tuple-element.206), kind=kOutput, calls=%fused_computation.11.clone.clone.1 | convolution fusion | flops 7252474368 | bytes 6307840 | tf_op jit(solution)/shard_map/while/body/eval_jaxpr/id,jd->ij/dot_general | solution.py:24
  368.2 10.9 %fusion.38 = f32[1536]{0:T(1024)S(1)} fusion(f32[1536,768]{1,0:T(8,128)} %get-tuple-element.205, f32[12,512,768]{2,1,0:T(8,128)} %get-tuple-element.204, s32[]{:T(128)} %get-tuple-element.191, pred[1536]{0:T(1024)(128)(4,1)S(1)} %broadcast_compare_fusion.3, s32[512]{0:T(512)S(1)} %bitcast.50, s32[1536]{0:T(1024)S(1)} %get-tuple-element.206), kind=kOutput, calls=%fused_computation.11.clone.clone.1 | convolution fusion | flops 7252474368 | bytes 6307840 | tf_op jit(solution)/shard_map/while/body/eval_jaxpr/id,jd->ij/dot_general | solution.py:24
  379.2 10.9 %fusion.38 = f32[1536]{0:T(1024)S(1)} fusion(f32[1536,768]{1,0:T(8,128)} %get-tuple-element.205, f32[12,512,768]{2,1,0:T(8,128)} %get-tuple-element.204, s32[]{:T(128)} %get-tuple-element.191, pred[1536]{0:T(1024)(128)(4,1)S(1)} %broadcast_compare_fusion.3, s32[512]{0:T(512)S(1)} %bitcast.50, s32[1536]{0:T(1024)S(1)} %get-tuple-element.206), kind=kOutput, calls=%fused_computation.11.clone.clone.1 | convolution fusion | flops 7252474368 | bytes 6307840 | tf_op jit(solution)/shard_map/while/body/eval_jaxpr/id,jd->ij/dot_general | solution.py:24
  390.2 10.9 %fusion.38 = f32[1536]{0:T(1024)S(1)} fusion(f32[1536,768]{1,0:T(8,128)} %get-tuple-element.205, f32[12,512,768]{2,1,0:T(8,128)} %get-tuple-element.204, s32[]{:T(128)} %get-tuple-element.191, pred[1536]{0:T(1024)(128)(4,1)S(1)} %broadcast_compare_fusion.3, s32[512]{0:T(512)S(1)} %bitcast.50, s32[1536]{0:T(1024)S(1)} %get-tuple-element.206), kind=kOutput, calls=%fused_computation.11.clone.clone.1 | convolution fusion | flops 7252474368 | bytes 6307840 | tf_op jit(solution)/shard_map/while/body/eval_jaxpr/id,jd->ij/dot_general | solution.py:24
  401.8 7.8 %all-to-all-start.2 = ((f32[32,1,48]{2,1,0:T(1,128)}), f32[32,1,48]{2,1,0:T(1,128)S(1)}, u32[]{:S(2)}, u32[]{:S(2)}) async-start(f32[32,1,48]{2,1,0:T(1,128)} %all_to_all.21), calls=%async_computation.2 | async-start | bytes 32768 | tf_op jit(solution)/shard_map/all_to_all | solution.py:90
  410.3 6.2 %all-to-all-done.2 = f32[32,1,48]{2,1,0:T(1,128)S(1)} async-done(((f32[32,1,48]{2,1,0:T(1,128)}), f32[32,1,48]{2,1,0:T(1,128)S(1)}, u32[]{:S(2)}, u32[]{:S(2)}) %all-to-all-start.2) | async-done | bytes 6176 | tf_op jit(solution)/shard_map/all_to_all | solution.py:90
  417.8 4.5 %gather_fusion = f32[768]{0:T(1024)S(1)} fusion(f32[1536]{0:T(1024)S(1)} %reshape.115, s32[1024]{0:T(1024)S(1)} %pad_clamp_fusion), kind=kCustom, calls=%fused_computation | custom fusion | bytes 9216 | tf_op jit(solution)/shard_map/gather | solution.py:93
  422.3 3.9 scatter_custom_fusion.2
  (81 shorter events, 6.9 us)
Async XLA Ops:
  8.0 5.3 %copy-start = (f32[768,768]{1,0:T(8,128)S(1)}, f32[768,768]{1,0:T(8,128)}, u32[]{:S(2)}) copy-start(f32[768,768]{1,0:T(8,128)} %param.6) | copy-start | bytes 7077892
  23.1 9.7 %copy-start.2 = (s32[512]{0:T(512)S(1)}, s32[512]{0:T(512)}, u32[]{:S(2)}) copy-start(s32[512]{0:T(512)} %param.8) | copy-start | bytes 6148
  23.1 10.1 %copy-start.3 = (s32[768]{0:T(1024)S(1)}, s32[768]{0:T(1024)}, u32[]{:S(2)}) copy-start(s32[768]{0:T(1024)} %param.7) | copy-start | bytes 9220
  23.1 69.2 %all-to-all-start.1 = ((f32[32,48,768]{2,1,0:T(8,128)}), f32[32,48,768]{2,1,0:T(8,128)}, u32[]{:S(2)}, u32[]{:S(2)}) async-start(f32[32,48,768]{2,1,0:T(8,128)} %bitcast.46), calls=%async_computation.1 | async-start | bytes 9437184 | tf_op jit(solution)/shard_map/all_to_all | solution.py:71
  32.7 84.8 %reduce-scatter.2.cloned.1.call-start = ((), (), s32[]{:S(2)}) async-start(), calls=%async_computation.5 | async-start | bytes 1622016 | tf_op jit(solution)/shard_map/reduce_scatter | solution.py:108
  37.0 232.5 %all-gather.3.cloned.1.call-start = ((), (), s32[]{:S(2)}) async-start(), calls=%async_computation.4 | async-start | bytes 23592960 | tf_op jit(solution)/shard_map/all_gather | solution.py:87
  92.3 26.4 %copy-start.4 = (s32[768]{0:T(1024)S(1)}, s32[768]{0:T(1024)}, u32[]{:S(2)}) copy-start(s32[768]{0:T(1024)} %param.9) | copy-start | bytes 9220
  96.4 29.1 %all-to-all-start = ((s32[32,1,48]{2,1,0:T(1,128)}), s32[32,1,48]{2,1,0:T(1,128)S(1)}, u32[]{:S(2)}, u32[]{:S(2)}) async-start(s32[32,1,48]{2,1,0:T(1,128)} %all_to_all.17), calls=%async_computation | async-start | bytes 32768 | tf_op jit(solution)/shard_map/all_to_all | solution.py:78
  117.5 4.6 %collective-permute-start = (f32[16,768]{1,0:T(8,128)}, f32[16,768]{1,0:T(8,128)S(1)}, u32[]{:S(2)}, u32[]{:S(2)}) collective-permute-start(f32[16,768]{1,0:T(8,128)} %reduce-scatter.2.cloned.1.call-done), channel_id=1, source_target_pairs={{0,32},{32,0},{64,96},{96,64},{1,33},{33,1},{65,97},{97,65},{2,34}... | collective-permute-start | bytes 147464 | tf_op jit(solution)/shard_map/ppermute | solution.py:111
  122.8 14.5 %collective-permute-start.1 = (f32[16,768]{1,0:T(8,128)S(1)}, f32[16,768]{1,0:T(8,128)S(1)}, u32[]{:S(2)}, u32[]{:S(2)}) collective-permute-start(f32[16,768]{1,0:T(8,128)S(1)} %add.95), channel_id=1, source_target_pairs={{0,64},{32,96},{64,0},{96,32},{1,65},{33,97},{65,1},{97,33},{2,66}... | collective-permute-start | bytes 147464 | tf_op jit(solution)/shard_map/ppermute | solution.py:111
  125.5 143.9 %copy-start.1 = (s32[32,1,48]{2,1,0:T(1,128)}, s32[32,1,48]{2,1,0:T(1,128)S(1)}, u32[]{:S(2)}) copy-start(s32[32,1,48]{2,1,0:T(1,128)S(1)} %all-to-all-done) | copy-start | bytes 18436
  401.8 14.7 %all-to-all-start.2 = ((f32[32,1,48]{2,1,0:T(1,128)}), f32[32,1,48]{2,1,0:T(1,128)S(1)}, u32[]{:S(2)}, u32[]{:S(2)}) async-start(f32[32,1,48]{2,1,0:T(1,128)} %all_to_all.21), calls=%async_computation.2 | async-start | bytes 32768 | tf_op jit(solution)/shard_map/all_to_all | solution.py:90
Sparse Core Ops, SparseCore 0:
  37.1 80.2 reduce-scatter.1
Sparse Core Ops, SparseCore 1:
  92.4 177.0 all-gather.2
